TPU v7x, 512 devices: a whole 4x4x16 slice. The times are simulated.
512 devices in a mesh: seq: 64 (over y, z), mp: 8 (over x, core).
Axes of the slice: x: 4, y: 4, z: 16, core: 2. Of those that a mesh axis runs over, the one named last changes fastest.
Arguments:
- byte_states: bfloat16 [16384, 1024], P('seq'), may hold values from -6 to 6
- outer_gain: float32 [1024], replicated, may hold values from 0.1 to 1.9
- mamba_input: bfloat16 [1024, 1024], P(None, 'mp'), may hold values from -0.1875 to 0.1875
- mamba_step: bfloat16 [1024, 1024], P(None, 'mp'), may hold values from -0.1875 to 0.1875
- decay_rate: float32 [1024], P('mp'), as said below
- mixer_weight: bfloat16 [1024, 1024], P('mp'), may hold values from -0.1875 to 0.1875
- boundaries: int32 [64, 128], P('seq'), may hold values from 0 to 256, as said below
- span_counts: int32 [64], replicated, may hold values from 1 to 128, as said below
- up_weight: bfloat16 [1024, 4096], P('seq', 'mp'), may hold values from -0.1875 to 0.1875
- up_bias: float32 [4096], P('mp'), may hold values from -5 to 5
- inner_gain: float32 [4096], replicated, as said below
- query_weight: bfloat16 [4096, 4096], P('seq', 'mp'), as said below
- key_weight: bfloat16 [4096, 1024], P('seq', 'mp'), as said below
- value_weight: bfloat16 [4096, 1024], P('seq', 'mp'), may hold values from -0.09375 to 0.09375
- return_weight: bfloat16 [4096, 1024], P('mp'), may hold values from -0.09375 to 0.09375
Outputs:
- joined: bfloat16 [16384, 1024], P('seq', 'mp')
Inputs may be any that keep to these rules, and one draw needn't show every extreme that they name: `boundaries`: row s lists the spans of shard s: its first span_counts[s] entries rise strictly from 0 and are byte positions within the shard; each span runs to the next entry, the last to the shard's end; the other entries equal 256. `span_counts`: the counts sum to 4096; some shard has exactly 128 spans. `decay_rate`: Positive. `inner_gain`: Positive. `query_weight`: Finite. `key_weight`: Finite.
All inputs are finite; a program needn't handle non-finite values.
Results may differ from a plain program's by a relative error of at most 0.01.
Values may be sent and summed in bfloat16 or wider, within the bound.
A program may use at most 64 MiB of HBM per device.

v0:
```python
import math
import jax
import jax.numpy as jnp
from jax import lax
from jax.sharding import PartitionSpec as P

HEADS = 32
KV_HEADS = 8
HEAD = 128
eps = 1e-05
masked = -1e30
far_index = 1073741824


def prefix(value, axis, join, neutral):
    count, mine = (lax.axis_size(axis), lax.axis_index(axis))
    pieces = jax.tree.map(lambda part: lax.all_gather(part, axis), value)
    so_far = jax.tree.map(
        lambda part, zero: jnp.full_like(part, 0) + jnp.asarray(zero, part.dtype), value, neutral
    )

    def lap(position, so_far):
        longer = join(so_far, jax.tree.map(lambda part: part[position], pieces))
        return jax.tree.map(lambda new, old: jnp.where(position < mine, new, old), longer, so_far)

    return lax.fori_loop(0, count - 1, lap, so_far)


def rms_scale(values, gain):
    values = values.astype(jnp.float32)
    return values * lax.rsqrt(jnp.mean(values * values, axis=-1, keepdims=True) + eps) * gain


def combine_pairs(earlier, later):
    return (earlier[0] * later[0], later[0] * earlier[1] + later[1])


def pick_table(table, wanted, seq_ids):
    return jnp.sum(jnp.where(seq_ids[None, :] == wanted[:, None], table[None, :], 0), axis=1)


def block_size(piece_rows, shard_rows):
    limit = max(1, 1024 // shard_rows)
    pieces = max(1, piece_rows // shard_rows)
    best_size = 1
    for candidate in range(1, limit + 1):
        if pieces % candidate == 0:
            best_size = candidate
    return min(piece_rows, best_size * shard_rows)


def on_device(
    byte_states,
    outer_gain,
    mamba_input,
    mamba_step,
    decay_rate,
    mixer_weight,
    boundaries,
    span_counts,
    up_weight,
    up_bias,
    inner_gain,
    query_weight,
    key_weight,
    value_weight,
    return_weight,
):
    shards = lax.axis_size("seq")
    own_shard = lax.axis_index("seq")
    own_lane = lax.axis_index("mp")
    rows_here = byte_states.shape[0]
    capacity = boundaries.shape[1]
    column_count = mamba_input.shape[1]
    kv_local = key_weight.shape[1] // HEAD
    group_size = HEADS // KV_HEADS
    offsets = jnp.cumsum(span_counts) - span_counts
    seq_ids = jnp.arange(shards, dtype=jnp.int32)
    own_offset = jnp.sum(jnp.where(seq_ids == own_shard, offsets, 0))
    own_count = jnp.sum(jnp.where(seq_ids == own_shard, span_counts, 0))
    normed = rms_scale(byte_states, outer_gain).astype(jnp.bfloat16)
    inputs = jnp.dot(normed, mamba_input, preferred_element_type=jnp.float32)
    step_sizes = jax.nn.softplus(jnp.dot(normed, mamba_step, preferred_element_type=jnp.float32))
    rate_steps = step_sizes * decay_rate
    decays = jnp.exp(-rate_steps)
    drives = jnp.sqrt(-jnp.expm1(-2.0 * rate_steps)) * inputs
    through, local_states = lax.associative_scan(combine_pairs, (decays, drives), axis=0)
    starting = (jnp.ones((column_count,), jnp.float32), jnp.zeros((column_count,), jnp.float32))
    arriving = prefix((through[-1], local_states[-1]), "seq", combine_pairs, starting)
    states = (local_states + through * arriving[1][None, :]).astype(jnp.bfloat16)
    partial_value = jnp.dot(states, mixer_weight, preferred_element_type=jnp.float32)
    mixed_sum = lax.psum(partial_value, "mp")
    encoded = (byte_states.astype(jnp.float32) + mixed_sum).astype(jnp.bfloat16)
    skip_part = lax.dynamic_slice_in_dim(encoded, own_lane * column_count, column_count, 1)
    own_marks = boundaries[0]
    pooled = encoded[jnp.minimum(own_marks, rows_here - 1)]
    local_slot = jnp.arange(capacity, dtype=jnp.int32)
    query_index = jnp.where(local_slot < own_count, own_offset + local_slot, -1)
    columns = pooled
    widened_sum = jnp.dot(
        columns,
        lax.all_gather(up_weight, "seq", axis=0, tiled=True),
        preferred_element_type=jnp.float32,
    )
    widened_share = (widened_sum + up_bias[None, :]).astype(jnp.bfloat16)
    widened = lax.all_gather(widened_share, "mp", axis=1, tiled=True)
    inner_normed = rms_scale(widened, inner_gain).astype(jnp.bfloat16)
    columns = inner_normed
    query_part = jnp.dot(
        columns,
        lax.all_gather(query_weight, "seq", axis=0, tiled=True),
        preferred_element_type=jnp.float32,
    )
    key_part = jnp.dot(
        columns,
        lax.all_gather(key_weight, "seq", axis=0, tiled=True),
        preferred_element_type=jnp.float32,
    )
    value_part = jnp.dot(
        columns,
        lax.all_gather(value_weight, "seq", axis=0, tiled=True),
        preferred_element_type=jnp.float32,
    )
    queries = query_part.astype(jnp.bfloat16)
    key_rows = key_part.astype(jnp.bfloat16)
    value_rows = value_part.astype(jnp.bfloat16)
    query_count = queries.shape[0]
    grouped = (
        queries.reshape(query_count, kv_local, group_size, HEAD)
        .transpose(1, 0, 2, 3)
        .reshape(kv_local, query_count * group_size, HEAD)
    )
    row_index = jnp.repeat(query_index, group_size)
    shard_rows = key_rows.shape[0]
    score_scale = 1.0 / math.sqrt(HEAD)

    def key_index(whole_index):
        holder = whole_index // shard_rows
        within = whole_index % shard_rows
        holder_offset = pick_table(offsets, holder, seq_ids)
        holder_count = pick_table(span_counts, holder, seq_ids)
        return jnp.where(within < holder_count, holder_offset + within, far_index)

    def attend_block(running, key_block, value_block, index_block):
        row_peak, denominator, weighted = running
        scores = (
            jnp.einsum("hqd,khd->hqk", grouped, key_block, preferred_element_type=jnp.float32)
            * score_scale
        )
        scores = jnp.where(index_block[None, None, :] <= row_index[None, :, None], scores, masked)
        new_peak = jnp.maximum(row_peak, jnp.max(scores, axis=2))
        shrink = jnp.exp(row_peak - new_peak)
        lifted = jnp.exp(scores - new_peak[:, :, None])
        denominator = denominator * shrink + jnp.sum(lifted, axis=2)
        weighted = weighted * shrink[:, :, None] + jnp.einsum(
            "hqk,khd->hqd",
            lifted.astype(jnp.bfloat16),
            value_block,
            preferred_element_type=jnp.float32,
        )
        return (new_peak, denominator, weighted)

    query_total = query_count * group_size
    initial = (
        jnp.full((kv_local, query_total), masked, jnp.float32),
        jnp.zeros((kv_local, query_total), jnp.float32),
        jnp.zeros((kv_local, query_total, HEAD), jnp.float32),
    )
    key_piece = lax.all_gather(key_rows, "seq", axis=0, tiled=True)
    value_piece = lax.all_gather(value_rows, "seq", axis=0, tiled=True)
    piece_rows = key_piece.shape[0]
    block_rows = block_size(piece_rows, shard_rows)
    turn_count = piece_rows // block_rows
    key_blocks = key_piece.reshape(turn_count, block_rows, kv_local, HEAD)
    value_blocks = value_piece.reshape(turn_count, block_rows, kv_local, HEAD)

    def one_turn(turn_index, inner_running):
        whole_index = turn_index * block_rows + jnp.arange(block_rows, dtype=jnp.int32)
        return attend_block(
            inner_running, key_blocks[turn_index], value_blocks[turn_index], key_index(whole_index)
        )

    row_peak, denominator, weighted = lax.fori_loop(0, turn_count, one_turn, initial)
    attended = (weighted / denominator[:, :, None]).astype(jnp.bfloat16)
    attended = (
        attended.reshape(kv_local, query_count, group_size, HEAD)
        .transpose(1, 0, 2, 3)
        .reshape(query_count, kv_local * group_size * HEAD)
    )
    projected = jnp.dot(attended, return_weight, preferred_element_type=jnp.float32)
    returned = lax.psum_scatter(
        projected.astype(jnp.bfloat16), "mp", scatter_dimension=1, tiled=True
    )
    positions = jnp.arange(rows_here, dtype=jnp.int32)
    live_slots = jnp.arange(capacity, dtype=jnp.int32) < own_count
    passed = jnp.sum(
        ((own_marks[None, :] <= positions[:, None]) & live_slots[None, :]).astype(jnp.int32), axis=1
    )
    return (skip_part.astype(jnp.float32) + returned[passed - 1].astype(jnp.float32)).astype(
        jnp.bfloat16
    )


def solution(mesh):
    in_specs = (
        P("seq", None),
        P(),
        P(None, "mp"),
        P(None, "mp"),
        P("mp"),
        P("mp", None),
        P("seq", None),
        P(),
        P("seq", "mp"),
        P("mp"),
        P(),
        P("seq", "mp"),
        P("seq", "mp"),
        P("seq", "mp"),
        P("mp", None),
    )
    out_specs = P("seq", "mp")
    return jax.shard_map(
        on_device, mesh=mesh, in_specs=in_specs, out_specs=out_specs, check_vma=False
    )
```

profile of v0, /device:TPU:8, one launch (start us, length us, event | category | flops | bytes accessed | tf_op | source)
XLA Modules:
  0.0 1139.2 jit_solution(18261109659851616036)
XLA Ops:
  8.8 1.5 negate_exponential_fusion
  12.6 79.6 %all-gather.1 = f32[64,1,128]{2,1,0:T(1,128)S(1)} all-gather(f32[1,1,128]{2,1,0:T(1,128)S(1)} %add_bitcast_fusion), channel_id=1, replica_groups=mesh['seq'=64,'mp'=8] {'seq'}, dimensions={0}, use_global_device_ids=true | all-gather | bytes 33280 | tf_op jit(solution)/shard_map/all_gather | solution.py:17
  92.3 73.3 %all-gather = f32[64,1,128]{2,1,0:T(1,128)S(1)} all-gather(f32[1,1,128]{2,1,0:T(1,128)S(1)} %add_bitcast_fusion.1), channel_id=1, replica_groups=mesh['seq'=64,'mp'=8] {'seq'}, dimensions={0}, use_global_device_ids=true | all-gather | bytes 33280 | tf_op jit(solution)/shard_map/all_gather | solution.py:17
  165.6 2.6 while.34
  170.2 73.0 %all-reduce.34.cloned.1.call-done = f32[256,1024]{1,0:T(8,128)} async-done(((f32[256,1024]{1,0:T(8,128)}), f32[256,1024]{1,0:T(8,128)}) %all-reduce.34.cloned.1.call-update) | async-done | bytes 1048592 | tf_op jit(solution)/shard_map/psum | solution.py:92
  245.5 61.3 %all-gather.10.cloned.1.call-done = bf16[1024,512]{1,0:T(8,128)(2,1)} async-done(((bf16[16,512]{1,0:T(8,128)(2,1)}), bf16[1024,512]{1,0:T(8,128)(2,1)}) %all-gather.10.cloned.1.call-update) | async-done | bytes 1048592 | tf_op jit(solution)/shard_map/all_gather | solution.py:102
  306.7 2.2 fusion.31
  310.9 26.2 %all-gather.12.cloned.1.call-done = bf16[128,4096]{1,0:T(8,128)(2,1)} async-done(((bf16[128,512]{1,0:T(8,128)(2,1)}), bf16[128,4096]{1,0:T(8,128)(2,1)}) %all-gather.12.cloned.1.call-update) | async-done | bytes 1048592 | tf_op jit(solution)/shard_map/all_gather | solution.py:106
  337.1 1.6 fusion.28
  338.8 140.2 %all-gather.20.cloned.1.call-done = bf16[4096,128]{1,0:T(8,128)(2,1)} async-done(((bf16[64,128]{1,0:T(8,128)(2,1)}), bf16[4096,128]{1,0:T(8,128)(2,1)}) %all-gather.20.cloned.1.call-update) | async-done | bytes 1048592 | tf_op jit(solution)/shard_map/all_gather | solution.py:121
  478.9 2.7 convolution_convert_fusion.2
  481.7 136.0 %all-gather.14.cloned.1.call-done = bf16[4096,128]{1,0:T(8,128)(2,1)} async-done(((bf16[64,128]{1,0:T(8,128)(2,1)}), bf16[4096,128]{1,0:T(8,128)(2,1)}) %all-gather.14.cloned.1.call-update) | async-done | bytes 1048592 | tf_op jit(solution)/shard_map/all_gather | solution.py:116
  617.7 2.3 convolution_convert_fusion.3
  622.5 1.9 add_select_fusion.3
  625.1 137.2 %all-gather.18.cloned.1.call-done = bf16[4096,512]{1,0:T(8,128)(2,1)} async-done(((bf16[64,512]{1,0:T(8,128)(2,1)}), bf16[4096,512]{1,0:T(8,128)(2,1)}) %all-gather.18.cloned.1.call-update) | async-done | bytes 4194320 | tf_op jit(solution)/shard_map/all_gather | solution.py:111
  762.2 3.0 convolution_convert_fusion.1
  765.3 135.9 %all-gather.22.cloned.1.call-done = bf16[8192,128]{1,0:T(8,128)(2,1)} async-done(((bf16[128,128]{1,0:T(8,128)(2,1)}), bf16[8192,128]{1,0:T(8,128)(2,1)}) %all-gather.22.cloned.1.call-update) | async-done | bytes 2097168 | tf_op jit(solution)/shard_map/all_gather | solution.py:170
  901.2 140.0 %all-gather.16.cloned.1.call-done = bf16[8192,128]{1,0:T(8,128)(2,1)} async-done(((bf16[128,128]{1,0:T(8,128)(2,1)}), bf16[8192,128]{1,0:T(8,128)(2,1)}) %all-gather.16.cloned.1.call-update) | async-done | bytes 2097168 | tf_op jit(solution)/shard_map/all_gather | solution.py:169
  1041.2 50.0 %while.35 = (s32[]{:T(128)}, f32[1,512]{1,0:T(1,128)S(1)}, f32[1,512]{1,0:T(1,128)S(1)}, f32[1,512,128]{2,1,0:T(8,128)S(1)}, s32[64]{0:T(128)S(1)}, /*index=5*/s...) while((s32[]{:T(128)}, f32[1,512]{1,0:T(1,128)S(1)}, ...), condition=%wide.region_13.14_spmd.clone, body=%wide.region_8.13_spmd.clone.sunk | while | flops 273186304 | bytes 7548097 | solution.py:183
  1042.9 2.0 fusion.78
  1049.2 2.0 fusion.78
  1055.4 2.0 fusion.78
  1058.5 1.5 fusion.82
  1061.7 2.0 fusion.78
  1064.7 1.5 fusion.82
  1067.9 2.0 fusion.78
  1071.0 1.5 fusion.82
  1074.1 2.0 fusion.78
  1080.4 2.0 fusion.78
  1086.6 2.0 fusion.78
  1092.7 35.8 %reduce-scatter.4.cloned.1.call-done = bf16[128,128]{1,0:T(8,128)(2,1)} async-done(((bf16[1024,128]{1,0:T(8,128)(2,1)}), bf16[128,128]{1,0:T(8,128)(2,1)}) %reduce-scatter.4.cloned.1.call-update) | async-done | bytes 32784
  1130.3 1.5 add_convert_fusion
  (351 shorter events, 45.8 us)
Async XLA Ops:
  7.4 1084.1 %copy-start = (bf16[512,1024]{1,0:T(8,128)(2,1)S(1)}, bf16[512,1024]{1,0:T(8,128)(2,1)}, u32[]{:S(2)}) copy-start(bf16[512,1024]{1,0:T(8,128)(2,1)} %param.33) | copy-start | bytes 3145732
  7.4 3.0 copy-start.2
  7.4 3.0 copy-start.12
  7.4 3.0 copy-start.10
  7.4 235.8 %all-reduce.34.cloned.1.call-start = ((), (), s32[]{:S(2)}) async-start(), calls=%async_computation.1 | async-start | bytes 2097152 | tf_op jit(solution)/shard_map/psum | solution.py:92
  11.7 156.5 %copy-start.4 = (bf16[128,1024]{1,0:T(8,128)(2,1)S(1)}, bf16[128,1024]{1,0:T(8,128)(2,1)}, u32[]{:S(2)}) copy-start(bf16[128,1024]{1,0:T(8,128)(2,1)} %param.24) | copy-start | bytes 786436
  12.5 157.6 %copy-start.9 = (s32[1,128]{1,0:T(1,128)S(1)}, s32[1,128]{1,0:T(1,128)}, u32[]{:S(2)}) copy-start(s32[1,128]{1,0:T(1,128)} %param.25) | copy-start | bytes 1540
  169.5 137.2 %all-gather.10.cloned.1.call-start = ((), (), s32[]{:S(2)}) async-start(), calls=%async_computation.2 | async-start | bytes 1064960 | tf_op jit(solution)/shard_map/all_gather | solution.py:102
  170.1 167.0 %all-gather.12.cloned.1.call-start = ((), (), s32[]{:S(2)}) async-start(), calls=%async_computation.3 | async-start | bytes 1179648 | tf_op jit(solution)/shard_map/all_gather | solution.py:106
  170.2 136.5 %copy-start.8 = (f32[512]{0:T(512)S(1)}, f32[512]{0:T(512)}, u32[]{:S(2)}) copy-start(f32[512]{0:T(512)} %param.28) | copy-start | bytes 6148
  244.6 94.2 %copy-start.1 = (bf16[256,1024]{1,0:T(8,128)(2,1)}, bf16[256,1024]{1,0:T(8,128)(2,1)S(1)}, u32[]{:S(2)}) copy-start(bf16[256,1024]{1,0:T(8,128)(2,1)S(1)} %fusion.35) | copy-start | bytes 1572868
  244.6 234.3 %copy-start.11 = (f32[4096]{0:T(1024)S(1)}, f32[4096]{0:T(1024)}, u32[]{:S(2)}) copy-start(f32[4096]{0:T(1024)} %param.29) | copy-start | bytes 49156
  309.0 170.0 %all-gather.20.cloned.1.call-start = ((), (), s32[]{:S(2)}) async-start(), calls=%async_computation.7 | async-start | bytes 1064960 | tf_op jit(solution)/shard_map/all_gather | solution.py:121
  309.7 308.0 %all-gather.14.cloned.1.call-start = ((), (), s32[]{:S(2)}) async-start(), calls=%async_computation.4 | async-start | bytes 1064960 | tf_op jit(solution)/shard_map/all_gather | solution.py:116
  310.3 452.0 %all-gather.18.cloned.1.call-start = ((), (), s32[]{:S(2)}) async-start(), calls=%async_computation.6 | async-start | bytes 4259840 | tf_op jit(solution)/shard_map/all_gather | solution.py:111
  310.9 590.4 %all-gather.22.cloned.1.call-start = ((), (), s32[]{:S(2)}) async-start(), calls=%async_computation.8 | async-start | bytes 2129920 | tf_op jit(solution)/shard_map/all_gather | solution.py:170
  337.1 280.6 %copy-start.3 = (bf16[128,4096]{1,0:T(8,128)(2,1)S(1)}, bf16[128,4096]{1,0:T(8,128)(2,1)}, u32[]{:S(2)}) copy-start(bf16[128,4096]{1,0:T(8,128)(2,1)} %all-gather.12.cloned.1.call-done) | copy-start | bytes 3145732
  338.8 281.4 %copy-start.5 = (s32[64]{0:T(128)S(1)}, s32[64]{0:T(128)}, u32[]{:S(2)}) copy-start(s32[64]{0:T(128)} %param.26) | copy-start | bytes 772
  481.6 559.6 %all-gather.16.cloned.1.call-start = ((), (), s32[]{:S(2)}) async-start(), calls=%async_computation.5 | async-start | bytes 2129920 | tf_op jit(solution)/shard_map/all_gather | solution.py:169
  620.1 508.4 %reduce-scatter.4.cloned.1.call-start = ((), (), s32[]{:S(2)}) async-start(), calls=%async_computation.9 | async-start | bytes 294912
  1045.6 1.9 copy-start.6
  1051.8 1.9 copy-start.6
  1058.1 1.9 copy-start.6
  1064.3 1.9 copy-start.6
  1070.6 1.9 copy-start.6
  1076.8 1.9 copy-start.6
  1083.1 1.9 copy-start.6
  1089.3 1.9 copy-start.6
  1091.2 1.4 copy-start.7
Sparse Core Ops, SparseCore 0:
  169.7 73.5 all-reduce.33
  309.1 27.9 all-gather.11
  340.1 138.8 all-gather.19
  481.7 135.9 all-gather.13
  620.5 141.6 all-gather.17
  765.0 136.1 all-gather.21
  904.2 137.0 all-gather.15
  1092.8 35.7 reduce-scatter.3
Sparse Core Ops, SparseCore 1:
  173.0 133.7 all-gather.9
where the time goes:
time: 1140 us
  waiting for transfers between devices  888 us (78%)
  blocking collectives  153 us (13%)
  matrix products  41.2 us (4%)
  other arithmetic  27.3 us (2%)
  between operations  15.9 us (1%)
  local copies, waits for them, and re-layouts  11.6 us (1%)
    all_gather x2, blocking collectives, prefix(): pieces = jax.tree.map(lambda part: lax.all_gather(part, axis), value)  153 us
    all_gather x1, waiting for transfers between devices, on_device(): lax.all_gather(value_weight, 'seq', axis=0, tiled=True)  140 us
    all_gather x1, waiting for transfers between devices, on_device(): key_piece = lax.all_gather(key_rows, 'seq', axis=0, tiled=True)  140 us
    all_gather x1, waiting for transfers between devices, on_device(): lax.all_gather(query_weight, 'seq', axis=0, tiled=True)  137 us
    all_gather x1, waiting for transfers between devices, on_device(): lax.all_gather(key_weight, 'seq', axis=0, tiled=True)  136 us
    all_gather x1, waiting for transfers between devices, on_device(): value_piece = lax.all_gather(value_rows, 'seq', axis=0, tiled=True)  136 us
    psum x1, waiting for transfers between devices, on_device(): mixed_sum = lax.psum(partial_value, 'mp')  73 us
    all_gather x1, waiting for transfers between devices, on_device(): lax.all_gather(up_weight, 'seq', axis=0, tiled=True)  61.3 us
  transfers between devices with their start and end apart: 9, of which 9 were waited for; matrix products, arithmetic and copies ran while one was open for 1% of the time, Pallas kernels for 0%

commit v1 on v0

--- a/solution.py
+++ b/solution.py
@@ -10,6 +10,12 @@
 eps = 1e-05
 masked = -1e30
 far_index = 1073741824
+
+
+def gather_and_add(block, mesh_axis):
+    parts = lax.all_gather(block, mesh_axis, axis=0, tiled=False)
+    total = parts.sum(axis=0)
+    return total
 
 
 def prefix(value, axis, join, neutral):
@@ -89,7 +95,7 @@
     arriving = prefix((through[-1], local_states[-1]), "seq", combine_pairs, starting)
     states = (local_states + through * arriving[1][None, :]).astype(jnp.bfloat16)
     partial_value = jnp.dot(states, mixer_weight, preferred_element_type=jnp.float32)
-    mixed_sum = lax.psum(partial_value, "mp")
+    mixed_sum = gather_and_add(partial_value, "mp")
     encoded = (byte_states.astype(jnp.float32) + mixed_sum).astype(jnp.bfloat16)
     skip_part = lax.dynamic_slice_in_dim(encoded, own_lane * column_count, column_count, 1)
     own_marks = boundaries[0]

time: 1140 us -> 1200 us (1.053)
  waiting for transfers between devices: 888 us -> 942 us
    all_gather x1, waiting for transfers between devices: 61.3 us -> 137 us  [on_device(): lax.all_gather(up_weight, 'seq', axis=0, tiled=True)]
    psum x1 -> x0, waiting for transfers between devices: 73 us -> none  [on_device(): mixed_sum = lax.psum(partial_value, 'mp')]
    all_gather x0 -> x1, waiting for transfers between devices: none -> 51.4 us  [gather_and_add(): parts = lax.all_gather(block, mesh_axis, axis=0, tiled=False)]
  transfers between devices with their start and end apart: 9 -> 9, of which waited for: 9 -> 9; matrix products, arithmetic and copies ran while one was open for 1% -> 2% of each run, Pallas kernels for 0% -> 0%
where the time goes in v1:
time: 1200 us; the launch traced here: 1190 us
  waiting for transfers between devices  942 us (78%)
  blocking collectives  153 us (13%)
  matrix products  41.2 us (3%)
  other arithmetic  29.8 us (2%)
  between operations  14.2 us (1%)
    all_gather x2, blocking collectives, prefix(): pieces = jax.tree.map(lambda part: lax.all_gather(part, axis), value)  153 us
    all_gather x1, waiting for transfers between devices, on_device(): lax.all_gather(value_weight, 'seq', axis=0, tiled=True)  140 us
    all_gather x1, waiting for transfers between devices, on_device(): key_piece = lax.all_gather(key_rows, 'seq', axis=0, tiled=True)  140 us
    all_gather x1, waiting for transfers between devices, on_device(): lax.all_gather(query_weight, 'seq', axis=0, tiled=True)  138 us
    all_gather x1, waiting for transfers between devices, on_device(): lax.all_gather(up_weight, 'seq', axis=0, tiled=True)  137 us
    all_gather x1, waiting for transfers between devices, on_device(): value_piece = lax.all_gather(value_rows, 'seq', axis=0, tiled=True)  136 us
    all_gather x1, waiting for transfers between devices, on_device(): lax.all_gather(key_weight, 'seq', axis=0, tiled=True)  136 us
    all_gather x1, waiting for transfers between devices, gather_and_add(): parts = lax.all_gather(block, mesh_axis, axis=0, tiled=False)  51.4 us
  transfers between devices with their start and end apart: 9, of which 9 were waited for; matrix products, arithmetic and copies ran while one was open for 2% of the time, Pallas kernels for 0%

profile of v1, /device:TPU:8, one launch (start us, length us, event | category | flops | bytes accessed | tf_op | source)
XLA Modules:
  0.0 1193.9 jit_solution(5243397036859866671)
XLA Ops:
  7.9 1.5 negate_exponential_fusion
  11.8 79.6 %all-gather.2 = f32[64,1,128]{2,1,0:T(1,128)S(1)} all-gather(f32[1,1,128]{2,1,0:T(1,128)S(1)} %add_bitcast_fusion), channel_id=1, replica_groups=mesh['seq'=64,'mp'=8] {'seq'}, dimensions={0}, use_global_device_ids=true | all-gather | bytes 33280 | tf_op jit(solution)/shard_map/all_gather | solution.py:23
  91.5 73.3 %all-gather.1 = f32[64,1,128]{2,1,0:T(1,128)S(1)} all-gather(f32[1,1,128]{2,1,0:T(1,128)S(1)} %add_bitcast_fusion.1), channel_id=1, replica_groups=mesh['seq'=64,'mp'=8] {'seq'}, dimensions={0}, use_global_device_ids=true | all-gather | bytes 33280 | tf_op jit(solution)/shard_map/all_gather | solution.py:23
  164.8 2.6 while.34
  169.5 51.4 %all-gather.26.cloned.1.call-done = f32[2048,1024]{1,0:T(8,128)} async-done(((f32[256,1024]{1,0:T(8,128)}), f32[2048,1024]{1,0:T(8,128)}) %all-gather.26.cloned.1.call-update) | async-done | bytes 8388624 | tf_op jit(solution)/shard_map/all_gather | solution.py:16
  221.0 4.4 reduce_sum.100
  226.4 136.7 %all-gather.12.cloned.1.call-done = bf16[1024,512]{1,0:T(8,128)(2,1)} async-done(((bf16[16,512]{1,0:T(8,128)(2,1)}), bf16[1024,512]{1,0:T(8,128)(2,1)}) %all-gather.12.cloned.1.call-update) | async-done | bytes 1048592 | tf_op jit(solution)/shard_map/all_gather | solution.py:108
  363.1 2.2 fusion.31
  367.1 26.3 %all-gather.14.cloned.1.call-done = bf16[128,4096]{1,0:T(8,128)(2,1)} async-done(((bf16[128,512]{1,0:T(8,128)(2,1)}), bf16[128,4096]{1,0:T(8,128)(2,1)}) %all-gather.14.cloned.1.call-update) | async-done | bytes 1048592 | tf_op jit(solution)/shard_map/all_gather | solution.py:112
  393.4 1.6 fusion.28
  395.1 140.0 %all-gather.22.cloned.1.call-done = bf16[4096,128]{1,0:T(8,128)(2,1)} async-done(((bf16[64,128]{1,0:T(8,128)(2,1)}), bf16[4096,128]{1,0:T(8,128)(2,1)}) %all-gather.22.cloned.1.call-update) | async-done | bytes 1048592 | tf_op jit(solution)/shard_map/all_gather | solution.py:127
  535.1 2.7 convolution_convert_fusion.2
  537.8 136.0 %all-gather.16.cloned.1.call-done = bf16[4096,128]{1,0:T(8,128)(2,1)} async-done(((bf16[64,128]{1,0:T(8,128)(2,1)}), bf16[4096,128]{1,0:T(8,128)(2,1)}) %all-gather.16.cloned.1.call-update) | async-done | bytes 1048592 | tf_op jit(solution)/shard_map/all_gather | solution.py:122
  673.9 2.4 convolution_convert_fusion.3
  678.5 1.7 add_select_fusion.3
  680.9 137.5 %all-gather.20.cloned.1.call-done = bf16[4096,512]{1,0:T(8,128)(2,1)} async-done(((bf16[64,512]{1,0:T(8,128)(2,1)}), bf16[4096,512]{1,0:T(8,128)(2,1)}) %all-gather.20.cloned.1.call-update) | async-done | bytes 4194320 | tf_op jit(solution)/shard_map/all_gather | solution.py:117
  818.4 2.9 convolution_convert_fusion.1
  821.4 136.1 %all-gather.24.cloned.1.call-done = bf16[8192,128]{1,0:T(8,128)(2,1)} async-done(((bf16[128,128]{1,0:T(8,128)(2,1)}), bf16[8192,128]{1,0:T(8,128)(2,1)}) %all-gather.24.cloned.1.call-update) | async-done | bytes 2097168 | tf_op jit(solution)/shard_map/all_gather | solution.py:176
  957.5 140.0 %all-gather.18.cloned.1.call-done = bf16[8192,128]{1,0:T(8,128)(2,1)} async-done(((bf16[128,128]{1,0:T(8,128)(2,1)}), bf16[8192,128]{1,0:T(8,128)(2,1)}) %all-gather.18.cloned.1.call-update) | async-done | bytes 2097168 | tf_op jit(solution)/shard_map/all_gather | solution.py:175
  1097.5 49.3 %while.35 = (s32[]{:T(128)}, f32[1,512]{1,0:T(1,128)S(1)}, f32[1,512]{1,0:T(1,128)S(1)}, f32[1,512,128]{2,1,0:T(8,128)S(1)}, s32[64]{0:T(128)S(1)}, /*index=5*/s...) while((s32[]{:T(128)}, f32[1,512]{1,0:T(1,128)S(1)}, ...), condition=%wide.region_13.14_spmd.clone, body=%wide.region_8.13_spmd.clone.sunk | while | flops 273186304 | bytes 7548097 | solution.py:189
  1099.1 2.0 fusion.78
  1105.3 2.0 fusion.78
  1111.5 2.0 fusion.78
  1114.5 1.5 fusion.82
  1117.6 2.0 fusion.78
  1123.8 2.0 fusion.78
  1130.0 2.0 fusion.78
  1133.0 1.5 fusion.82
  1136.1 2.0 fusion.78
  1142.3 2.0 fusion.78
  1148.3 35.8 %reduce-scatter.4.cloned.1.call-done = bf16[128,128]{1,0:T(8,128)(2,1)} async-done(((bf16[1024,128]{1,0:T(8,128)(2,1)}), bf16[128,128]{1,0:T(8,128)(2,1)}) %reduce-scatter.4.cloned.1.call-update) | async-done | bytes 32784
  1185.9 1.5 add_convert_fusion
  (352 shorter events, 45.2 us)
Async XLA Ops:
  6.5 1140.6 %copy-start = (bf16[512,1024]{1,0:T(8,128)(2,1)S(1)}, bf16[512,1024]{1,0:T(8,128)(2,1)}, u32[]{:S(2)}) copy-start(bf16[512,1024]{1,0:T(8,128)(2,1)} %param.33) | copy-start | bytes 3145732
  6.5 3.0 copy-start.2
  6.5 3.0 copy-start.12
  6.5 3.0 copy-start.10
  6.5 214.4 %all-gather.26.cloned.1.call-start = ((), (), s32[]{:S(2)}) async-start(), calls=%async_computation.8 | async-start | bytes 9437184 | tf_op jit(solution)/shard_map/all_gather | solution.py:16
  10.9 156.5 %copy-start.4 = (bf16[128,1024]{1,0:T(8,128)(2,1)S(1)}, bf16[128,1024]{1,0:T(8,128)(2,1)}, u32[]{:S(2)}) copy-start(bf16[128,1024]{1,0:T(8,128)(2,1)} %param.24) | copy-start | bytes 786436
  11.7 157.8 %copy-start.9 = (s32[1,128]{1,0:T(1,128)S(1)}, s32[1,128]{1,0:T(1,128)}, u32[]{:S(2)}) copy-start(s32[1,128]{1,0:T(1,128)} %param.25) | copy-start | bytes 1540
  168.7 194.4 %all-gather.12.cloned.1.call-start = ((), (), s32[]{:S(2)}) async-start(), calls=%async_computation.1 | async-start | bytes 1064960 | tf_op jit(solution)/shard_map/all_gather | solution.py:108
  169.5 224.0 %all-gather.14.cloned.1.call-start = ((), (), s32[]{:S(2)}) async-start(), calls=%async_computation.2 | async-start | bytes 1179648 | tf_op jit(solution)/shard_map/all_gather | solution.py:112
  225.4 137.7 %copy-start.8 = (f32[512]{0:T(512)S(1)}, f32[512]{0:T(512)}, u32[]{:S(2)}) copy-start(f32[512]{0:T(512)} %param.28) | copy-start | bytes 6148
  225.5 169.5 %copy-start.1 = (bf16[256,1024]{1,0:T(8,128)(2,1)}, bf16[256,1024]{1,0:T(8,128)(2,1)S(1)}, u32[]{:S(2)}) copy-start(bf16[256,1024]{1,0:T(8,128)(2,1)S(1)} %fusion.35) | copy-start | bytes 1572868
  225.5 309.6 %copy-start.11 = (f32[4096]{0:T(1024)S(1)}, f32[4096]{0:T(1024)}, u32[]{:S(2)}) copy-start(f32[4096]{0:T(1024)} %param.29) | copy-start | bytes 49156
  365.3 169.8 %all-gather.22.cloned.1.call-start = ((), (), s32[]{:S(2)}) async-start(), calls=%async_computation.6 | async-start | bytes 1064960 | tf_op jit(solution)/shard_map/all_gather | solution.py:127
  365.9 308.0 %all-gather.16.cloned.1.call-start = ((), (), s32[]{:S(2)}) async-start(), calls=%async_computation.3 | async-start | bytes 1064960 | tf_op jit(solution)/shard_map/all_gather | solution.py:122
  366.5 451.9 %all-gather.20.cloned.1.call-start = ((), (), s32[]{:S(2)}) async-start(), calls=%async_computation.5 | async-start | bytes 4259840 | tf_op jit(solution)/shard_map/all_gather | solution.py:117
  367.1 590.5 %all-gather.24.cloned.1.call-start = ((), (), s32[]{:S(2)}) async-start(), calls=%async_computation.7 | async-start | bytes 2129920 | tf_op jit(solution)/shard_map/all_gather | solution.py:176
  393.4 280.4 %copy-start.3 = (bf16[128,4096]{1,0:T(8,128)(2,1)S(1)}, bf16[128,4096]{1,0:T(8,128)(2,1)}, u32[]{:S(2)}) copy-start(bf16[128,4096]{1,0:T(8,128)(2,1)} %all-gather.14.cloned.1.call-done) | copy-start | bytes 3145732
  395.1 281.3 %copy-start.5 = (s32[64]{0:T(128)S(1)}, s32[64]{0:T(128)}, u32[]{:S(2)}) copy-start(s32[64]{0:T(128)} %param.26) | copy-start | bytes 772
  537.8 559.7 %all-gather.18.cloned.1.call-start = ((), (), s32[]{:S(2)}) async-start(), calls=%async_computation.4 | async-start | bytes 2129920 | tf_op jit(solution)/shard_map/all_gather | solution.py:175
  676.3 507.9 %reduce-scatter.4.cloned.1.call-start = ((), (), s32[]{:S(2)}) async-start(), calls=%async_computation.9 | async-start | bytes 294912
  1101.8 1.9 copy-start.6
  1108.0 1.9 copy-start.6
  1114.1 1.9 copy-start.6
  1120.3 1.9 copy-start.6
  1126.5 1.9 copy-start.6
  1132.6 1.9 copy-start.6
  1138.8 1.9 copy-start.6
  1145.0 1.9 copy-start.6
  1146.8 1.5 copy-start.7
Sparse Core Ops, SparseCore 0:
  168.8 52.0 all-gather.25
  223.9 139.1 all-gather.11
  365.4 27.9 all-gather.13
  396.2 138.8 all-gather.21
  537.9 135.9 all-gather.15
  676.7 141.6 all-gather.19
  821.3 136.1 all-gather.23
  960.5 137.0 all-gather.17
  1148.4 35.7 reduce-scatter.3
